TPU v7x, 32 devices: a whole 2x2x4 slice. The times are simulated.
32 devices in a mesh: expert: 16 (over z, y, core), tensor: 2 (over x).
Axes of the slice: x: 2, y: 2, z: 4, core: 2. Of those that a mesh axis runs over, the one named last changes fastest.
Arguments:
- tokens: bfloat16 [18912, 768], P('expert'), may hold values from -6 to 6
- teacher: bfloat16 [18912, 768], P('expert'), may hold values from -12 to 12
- valid_flags: int32 [96], P('expert'), may hold values from 0 to 1, as said below
- routes: int32 [18912, 2], P('expert'), may hold values from 0 to 7, all different within a row; in each aligned block of 1182 rows (0 to 1181, 1182 to 2363, ...) at most 440 rows name the same one
- capacity: int32 [8], replicated, may hold values from 220 to 440, as said below
- norm_gains: bfloat16 [4, 768], replicated, may hold values from 0.5 to 1.5
- norm_biases: bfloat16 [4, 768], replicated, may hold values from -0.59765625 to 0.59765625
- attn_qkv: bfloat16 [2, 3, 768, 768], P(None, None, None, 'tensor'), may hold values from -0.21875 to 0.21875
- attn_out: bfloat16 [2, 768, 768], P(None, 'tensor'), may hold values from -1.75 to 1.75
- mlp_in: bfloat16 [768, 3072], P(None, 'tensor'), may hold values from -0.21875 to 0.21875
- mlp_out: bfloat16 [3072, 768], P('tensor'), may hold values from -0.109375 to 0.109375
- router: bfloat16 [768, 8], replicated, may hold values from -0.15625 to 0.15625
- expert_in: bfloat16 [16, 768, 1536], P('expert', None, 'tensor'), may hold values from -0.21875 to 0.21875
- expert_out: bfloat16 [16, 1536, 768], P('expert', 'tensor'), may hold values from -0.109375 to 0.109375
Outputs:
- activations: bfloat16 [18912, 768], P('expert')
- input_grad: bfloat16 [18912, 768], P('expert')
- gain_grad: float32 [4, 768], P(None, 'expert')
- bias_grad: float32 [3, 768], P(None, 'expert')
- expert_norm_bias_grad: float32 [768], P('expert')
- qkv_grad: float32 [2, 3, 768, 768], P(None, None, 'expert', 'tensor')
- out_proj_grad: float32 [2, 768, 768], P(None, 'tensor', 'expert')
- mlp_in_grad: float32 [768, 3072], P('expert', 'tensor')
- mlp_out_grad: float32 [3072, 768], P('tensor', 'expert')
- router_grad: float32 [768, 8], P('expert')
- expert_in_grad: float32 [16, 768, 1536], P('expert', None, 'tensor')
- expert_out_grad: float32 [16, 1536, 768], P('expert', 'tensor')
Inputs may be any that keep to these rules, and one draw needn't show every extreme that they name: `valid_flags`: 1 marks an image whose tokens count in the loss; image 0 is always valid. `routes`: the two experts of a token differ; among the rows of one index of expert no expert is named by more than 440 rows, and exactly 440 in some. `capacity`: exactly 440 for at least one expert.
All inputs are finite; a program needn't handle non-finite values.
Results may differ from a plain program's by a relative error of at most 0.035.
Values may be sent and summed in bfloat16 or wider, within the bound.
No kernel may reach another device: no remote copies, remote signals or barrier semaphores. Data moves between devices by JAX's collectives and lax.ppermute only.
A program may use at most 256 MiB of HBM per device.

v0:
```python
import jax
import jax.numpy as jnp
from jax import lax
from jax.sharding import PartitionSpec as P

HD = 64
SEQ = 197
IMG_DEV = 6
epsilon = 1e-06


def normalize(values, gain_row, bias_row):
    center = values - jnp.mean(values, axis=-1, keepdims=True)
    scaled = center * lax.rsqrt(jnp.mean(center * center, axis=-1, keepdims=True) + epsilon)
    return scaled * gain_row + bias_row


def norm_backward(values, gain_row, bias_row, grad_normed):
    pull_back = jax.vjp(normalize, values, gain_row, bias_row)[1]
    return pull_back(grad_normed)


def gelu_tanh(values):
    return jax.nn.gelu(values, approximate=True)


def tensor_total(partial_value):
    return lax.psum(partial_value.astype(jnp.bfloat16), "tensor").astype(jnp.float32)


def to_experts(buffer):
    doubled = jnp.repeat(buffer, 2, axis=0)
    arrived = lax.all_to_all(doubled, "expert", split_axis=0, concat_axis=0, tiled=True)
    return arrived


def from_experts(partial_value, experts):
    share_rows = lax.psum_scatter(
        partial_value.astype(jnp.bfloat16), "tensor", scatter_dimension=1, tiled=True
    )
    full_rows = lax.all_gather(share_rows, "tensor", axis=1, tiled=True)
    back_rows = lax.all_to_all(full_rows, "expert", split_axis=0, concat_axis=0, tiled=True)
    slots_each = back_rows.shape[1]
    halves = back_rows.reshape(experts, 2, slots_each, -1).astype(jnp.float32)
    return jnp.sum(halves, axis=1).reshape(experts * slots_each, -1)


def attend_forward(normed_low, qkv_weight, out_weight):
    packed = jnp.einsum(
        "td,sdc->stc", normed_low, qkv_weight, preferred_element_type=jnp.float32
    ).astype(jnp.bfloat16)
    heads_qkv = packed.reshape(3, IMG_DEV, SEQ, -1, HD)
    scores = jnp.einsum(
        "bqhe,bkhe->bhqk", heads_qkv[0], heads_qkv[1], preferred_element_type=jnp.float32
    ) * HD ** (-0.5)
    log_total = jax.nn.logsumexp(scores, axis=-1, keepdims=True)
    attn_probs = jnp.exp(scores - log_total).astype(jnp.bfloat16)
    mixed_rows = jnp.einsum(
        "bhqk,bkhe->bqhe", attn_probs, heads_qkv[2], preferred_element_type=jnp.float32
    )
    mixed_rows = mixed_rows.reshape(normed_low.shape[0], -1).astype(jnp.bfloat16)
    branch = jnp.dot(mixed_rows, out_weight, preferred_element_type=jnp.float32)
    return (branch, (packed, log_total, mixed_rows))


def attend_backward(grad_residual, normed_low, qkv_weight, out_weight, kept_state):
    packed, log_total, mixed_rows = kept_state
    grad_low = grad_residual.astype(jnp.bfloat16)
    grad_out = jnp.einsum("tc,td->cd", mixed_rows, grad_low, preferred_element_type=jnp.float32)
    heads_qkv = packed.reshape(3, IMG_DEV, SEQ, -1, HD)
    grad_mixed = jnp.einsum("td,cd->tc", grad_low, out_weight, preferred_element_type=jnp.float32)
    grad_mixed = grad_mixed.astype(jnp.bfloat16).reshape(heads_qkv.shape[1:])
    scores = jnp.einsum(
        "bqhe,bkhe->bhqk", heads_qkv[0], heads_qkv[1], preferred_element_type=jnp.float32
    ) * HD ** (-0.5)
    attn_probs = jnp.exp(scores - log_total)
    grad_probs = jnp.einsum(
        "bqhe,bkhe->bhqk", grad_mixed, heads_qkv[2], preferred_element_type=jnp.float32
    )
    grad_scores = attn_probs * (
        grad_probs - jnp.sum(grad_probs * attn_probs, axis=-1, keepdims=True)
    )
    grad_scores = grad_scores.astype(jnp.bfloat16)
    grad_query = jnp.einsum(
        "bhqk,bkhe->bqhe", grad_scores, heads_qkv[1], preferred_element_type=jnp.float32
    ) * HD ** (-0.5)
    grad_key = jnp.einsum(
        "bhqk,bqhe->bkhe", grad_scores, heads_qkv[0], preferred_element_type=jnp.float32
    ) * HD ** (-0.5)
    grad_value = jnp.einsum(
        "bhqk,bqhe->bkhe",
        attn_probs.astype(jnp.bfloat16),
        grad_mixed,
        preferred_element_type=jnp.float32,
    )
    grad_packed = (
        jnp.stack([grad_query, grad_key, grad_value]).reshape(packed.shape).astype(jnp.bfloat16)
    )
    grad_weight = jnp.einsum(
        "td,stc->sdc", normed_low, grad_packed, preferred_element_type=jnp.float32
    )
    grad_normed = jnp.einsum(
        "stc,sdc->td", grad_packed, qkv_weight, preferred_element_type=jnp.float32
    )
    return (grad_normed, grad_weight, grad_out)


def ffn_forward(rows_in, weight_in, weight_out):
    hidden = jnp.dot(rows_in, weight_in, preferred_element_type=jnp.float32)
    active = gelu_tanh(hidden).astype(jnp.bfloat16)
    return (jnp.dot(active, weight_out, preferred_element_type=jnp.float32), hidden, active)


def ffn_backward(grad_low, rows_in, weight_in, weight_out, hidden, active):
    grad_out = jnp.einsum("tf,td->fd", active, grad_low, preferred_element_type=jnp.float32)
    grad_active = jnp.einsum("td,fd->tf", grad_low, weight_out, preferred_element_type=jnp.float32)
    grad_hidden = jax.vjp(gelu_tanh, hidden)[1](grad_active)[0].astype(jnp.bfloat16)
    grad_in = jnp.einsum("td,tf->df", rows_in, grad_hidden, preferred_element_type=jnp.float32)
    grad_rows = jnp.einsum("tf,df->td", grad_hidden, weight_in, preferred_element_type=jnp.float32)
    return (grad_rows, grad_in, grad_out)


def body(
    tokens,
    teacher,
    valid_flags,
    routes,
    capacity,
    norm_gains,
    norm_biases,
    attn_qkv,
    attn_out,
    mlp_in,
    mlp_out,
    router,
    expert_in,
    expert_out,
):
    local_rows = tokens.shape[0]
    experts = router.shape[1]
    slots_each = 4 * (3 * local_rows // (4 * experts))
    all_slots = experts * slots_each
    owners = lax.axis_size("expert")
    gain_rows = norm_gains.astype(jnp.float32)
    bias_rows = norm_biases.astype(jnp.float32)
    local_count = SEQ * jnp.sum(valid_flags.astype(jnp.float32))
    valid_count = lax.psum(local_count, "expert")
    valid_rows = jnp.repeat(valid_flags.astype(jnp.float32), SEQ)[:, None]
    start_rows = tokens.astype(jnp.float32)
    normed_first = normalize(start_rows, gain_rows[0], bias_rows[0]).astype(jnp.bfloat16)
    branch, saved_first = attend_forward(normed_first, attn_qkv[0], attn_out[0])
    after_attn = start_rows + tensor_total(branch)
    normed_dense = normalize(after_attn, gain_rows[1], bias_rows[1]).astype(jnp.bfloat16)
    branch, dense_hidden, dense_active = ffn_forward(normed_dense, mlp_in, mlp_out)
    after_dense = after_attn + tensor_total(branch)
    normed_second = normalize(after_dense, gain_rows[2], bias_rows[2]).astype(jnp.bfloat16)
    branch, saved_second = attend_forward(normed_second, attn_qkv[1], attn_out[1])
    after_second = after_dense + tensor_total(branch)
    normed_expert = normalize(after_second, gain_rows[3], bias_rows[3]).astype(jnp.bfloat16)
    logits = jnp.dot(normed_expert, router, preferred_element_type=jnp.float32)
    picker = routes[:, :, None] == jnp.arange(experts, dtype=jnp.int32)[None, None, :]
    chosen = jnp.sum(jnp.where(picker, logits[:, None, :], 0.0), axis=2)
    gate_vals = jax.nn.softmax(chosen, axis=1)
    expert_of = jnp.concatenate([routes[:, 0], routes[:, 1]])
    onehot = (expert_of[:, None] == jnp.arange(experts, dtype=jnp.int32)[None, :]).astype(jnp.int32)
    earlier = jnp.cumsum(onehot, axis=0) - onehot
    position = jnp.sum(earlier * onehot, axis=1)
    kept_mask = position < jnp.sum(onehot * capacity[None, :], axis=1)
    slot_of = expert_of * slots_each + position
    pair_of = (
        jnp.full((all_slots,), -1, jnp.int32)
        .at[jnp.where(kept_mask, slot_of, all_slots)]
        .set(jnp.arange(2 * local_rows, dtype=jnp.int32), mode="drop")
    )
    slot_used = (pair_of >= 0)[:, None]
    pair_index = jnp.maximum(pair_of, 0)
    fetch_at = jnp.where(kept_mask, slot_of, 0)
    sent_rows = jnp.where(
        slot_used, normed_expert[pair_index % local_rows], jnp.zeros((), jnp.bfloat16)
    )
    rows_in = to_experts(sent_rows.reshape(experts, slots_each, -1)).reshape(
        owners * slots_each, -1
    )
    branch, expert_hidden, expert_active = ffn_forward(rows_in, expert_in[0], expert_out[0])
    merged = from_experts(branch.reshape(owners, slots_each, -1), experts)
    picked = jnp.where(kept_mask[:, None], merged[fetch_at], 0.0).reshape(2, local_rows, -1)
    gate_pairs = gate_vals.T[:, :, None]
    final_rows = after_second + jnp.sum(gate_pairs * picked, axis=0)
    grad_final = (
        local_rows * owners / valid_count * valid_rows * (final_rows - teacher.astype(jnp.float32))
    )
    grad_gates = jnp.sum(picked * grad_final[None], axis=2).T
    grad_pairs = (gate_pairs * grad_final[None]).astype(jnp.bfloat16).reshape(2 * local_rows, -1)
    grad_sent = jnp.where(slot_used, grad_pairs[pair_index], jnp.zeros((), jnp.bfloat16))
    grad_arrived = to_experts(grad_sent.reshape(experts, slots_each, -1)).reshape(
        owners * slots_each, -1
    )
    grad_rows, grad_expert_in, grad_expert_out = ffn_backward(
        grad_arrived, rows_in, expert_in[0], expert_out[0], expert_hidden, expert_active
    )
    grad_merged = from_experts(grad_rows.reshape(owners, slots_each, -1), experts)
    grad_taken = jnp.where(kept_mask[:, None], grad_merged[fetch_at], 0.0).reshape(
        2, local_rows, -1
    )
    grad_chosen = gate_vals * (grad_gates - jnp.sum(gate_vals * grad_gates, axis=1, keepdims=True))
    grad_logits = jnp.sum(jnp.where(picker, grad_chosen[:, :, None], 0.0), axis=1).astype(
        jnp.bfloat16
    )
    grad_router = jnp.einsum(
        "td,te->de", normed_expert, grad_logits, preferred_element_type=jnp.float32
    )
    grad_normed = jnp.sum(grad_taken, axis=0)
    grad_normed = grad_normed + jnp.einsum(
        "te,de->td", grad_logits, router, preferred_element_type=jnp.float32
    )
    grad_back, gain_four, bias_four = norm_backward(
        after_second, gain_rows[3], bias_rows[3], grad_normed
    )
    grad_second = grad_final + grad_back
    grad_part, qkv_two, out_two = attend_backward(
        grad_second, normed_second, attn_qkv[1], attn_out[1], saved_second
    )
    grad_back, gain_three, bias_three = norm_backward(
        after_dense, gain_rows[2], bias_rows[2], tensor_total(grad_part)
    )
    grad_dense = grad_second + grad_back
    grad_part, grad_mlp_in, grad_mlp_out = ffn_backward(
        grad_dense.astype(jnp.bfloat16), normed_dense, mlp_in, mlp_out, dense_hidden, dense_active
    )
    grad_back, gain_two, bias_two = norm_backward(
        after_attn, gain_rows[1], bias_rows[1], tensor_total(grad_part)
    )
    grad_attn = grad_dense + grad_back
    grad_part, qkv_one, out_one = attend_backward(
        grad_attn, normed_first, attn_qkv[0], attn_out[0], saved_first
    )
    grad_back, gain_one, bias_one = norm_backward(
        start_rows, gain_rows[0], bias_rows[0], tensor_total(grad_part)
    )
    grad_start = grad_attn + grad_back
    summed = (
        lax.psum_scatter(
            jnp.stack([gain_one, gain_two, gain_three, gain_four]),
            "expert",
            scatter_dimension=1,
            tiled=True,
        ),
        lax.psum_scatter(
            jnp.stack([bias_one, bias_two, bias_three]), "expert", scatter_dimension=1, tiled=True
        ),
        lax.psum_scatter(bias_four, "expert", scatter_dimension=0, tiled=True),
        lax.psum_scatter(jnp.stack([qkv_one, qkv_two]), "expert", scatter_dimension=2, tiled=True),
        lax.psum_scatter(jnp.stack([out_one, out_two]), "expert", scatter_dimension=2, tiled=True),
        lax.psum_scatter(grad_mlp_in, "expert", scatter_dimension=0, tiled=True),
        lax.psum_scatter(grad_mlp_out, "expert", scatter_dimension=1, tiled=True),
        lax.psum_scatter(grad_router, "expert", scatter_dimension=0, tiled=True),
    )
    return (
        final_rows.astype(jnp.bfloat16),
        grad_start.astype(jnp.bfloat16),
        summed[0],
        summed[1],
        summed[2],
        summed[3],
        summed[4],
        summed[5],
        summed[6],
        summed[7],
        grad_expert_in[None],
        grad_expert_out[None],
    )


def solution(mesh):
    in_specs = (
        P("expert", None),
        P("expert", None),
        P("expert"),
        P("expert", None),
        P(),
        P(),
        P(),
        P(None, None, None, "tensor"),
        P(None, "tensor", None),
        P(None, "tensor"),
        P("tensor", None),
        P(),
        P("expert", None, "tensor"),
        P("expert", "tensor", None),
    )
    out_specs = (
        P("expert", None),
        P("expert", None),
        P(None, "expert"),
        P(None, "expert"),
        P("expert"),
        P(None, None, "expert", "tensor"),
        P(None, "tensor", "expert"),
        P("expert", "tensor"),
        P("tensor", "expert"),
        P("expert", None),
        P("expert", None, "tensor"),
        P("expert", "tensor", None),
    )
    return jax.shard_map(body, mesh=mesh, in_specs=in_specs, out_specs=out_specs, check_vma=False)
```

profile of v0, /device:TPU:0, one launch (start us, length us, event | category | flops | bytes accessed | tf_op | source)
XLA Modules:
  0.0 2914.6 jit_solution(6737565340386454107)
XLA Ops:
  13.6 4.3 fusion.37
  57.4 59.4 %all-reduce.13.cloned.1.call-done = bf16[1182,768]{1,0:T(8,128)(2,1)} async-done(((bf16[1182,768]{1,0:T(8,128)(2,1)}), bf16[1182,768]{1,0:T(8,128)(2,1)}) %all-reduce.13.cloned.1.call-update) | async-done | bytes 1815568 | tf_op jit(solution)/shard_map/psum | solution.py:28
  127.7 5.4 convolution_convert_fusion.7
  133.9 56.3 %all-reduce.15.cloned.1.call-done = bf16[1182,768]{1,0:T(8,128)(2,1)} async-done(((bf16[1182,768]{1,0:T(8,128)(2,1)}), bf16[1182,768]{1,0:T(8,128)(2,1)}) %all-reduce.15.cloned.1.call-update) | async-done | bytes 1815568 | tf_op jit(solution)/shard_map/psum | solution.py:28
  201.2 4.4 reshape.525
  242.7 12.3 scatter_custom_fusion
  255.7 40.5 %all-reduce.17.cloned.1.call-done = bf16[1182,768]{1,0:T(8,128)(2,1)} async-done(((bf16[1182,768]{1,0:T(8,128)(2,1)}), bf16[1182,768]{1,0:T(8,128)(2,1)}) %all-reduce.17.cloned.1.call-update) | async-done | bytes 1815568 | tf_op jit(solution)/shard_map/psum | solution.py:28
  302.3 15.6 gather_fusion
  322.4 240.6 %all_to_all.20 = bf16[16,440,768]{2,1,0:T(8,128)(2,1)} all-to-all(bf16[16,440,768]{2,1,0:T(8,128)(2,1)S(1)} %bitcast.188), channel_id=1, replica_groups=mesh['expert'=16,'tensor'=2] {'expert'}, dimensions={0} | all-to-all | bytes 21626880 | tf_op jit(solution)/shard_map/all_to_all | solution.py:33
  562.9 20.0 multiply_convert_fusion
  582.9 13.2 convolution_convert_fusion.1
  596.1 9.1 copy.242
  605.2 125.0 %reduce-scatter.14.cloned.1.call-done = bf16[16,220,768]{2,0,1:T(8,128)(2,1)} async-done(((bf16[16,440,768]{2,0,1:T(8,128)(2,1)}), bf16[16,220,768]{2,0,1:T(8,128)(2,1)}) %reduce-scatter.14.cloned.1.call-update) | async-done | bytes 5406736 | tf_op jit(solution)/shard_map/reduce_scatter | solution.py:38
  730.3 134.6 %all-gather.3.cloned.1.call-done = bf16[16,440,768]{2,0,1:T(8,128)(2,1)} async-done(((bf16[16,220,768]{2,0,1:T(8,128)(2,1)}), bf16[16,440,768]{2,0,1:T(8,128)(2,1)}) %all-gather.3.cloned.1.call-update) | async-done | bytes 10813456 | tf_op jit(solution)/shard_map/all_gather | solution.py:41
  864.9 12.0 copy.243
  876.9 5.8 all-to-all-start.1
  884.0 211.2 %psum.52 = f32[]{:T(128)} all-reduce(f32[]{:T(128)S(6)} %mul_shard_map.3), channel_id=1, replica_groups=mesh['expert'=16,'tensor'=2] {'expert'}, use_global_device_ids=true, to_apply=%region_27.28 | all-reduce | flops 1 | bytes 8 | tf_op jit(solution)/shard_map/psum | solution.py:147
  1099.1 11.0 convert_reduce_fusion.1
  1110.1 14.3 gather_fusion.1
  1124.4 6.6 gather.23
  1142.8 6.6 mul.519
  1149.4 8.4 multiply_reduce_fusion.2
  1157.9 16.4 gather_fusion.2
  1178.7 279.8 %all_to_all.21 = bf16[16,440,768]{2,1,0:T(8,128)(2,1)S(1)} all-to-all(bf16[16,440,768]{2,1,0:T(8,128)(2,1)S(1)} %bitcast.189), channel_id=1, replica_groups=mesh['expert'=16,'tensor'=2] {'expert'}, dimensions={0} | all-to-all | bytes 21626880 | tf_op jit(solution)/shard_map/all_to_all | solution.py:33
  1458.5 28.1 fusion.6
  1486.6 11.8 convolution_convert_fusion
  1498.5 9.2 copy.246
  1507.7 125.0 %reduce-scatter.16.cloned.1.call-done = bf16[16,220,768]{2,0,1:T(8,128)(2,1)} async-done(((bf16[16,440,768]{2,0,1:T(8,128)(2,1)}), bf16[16,220,768]{2,0,1:T(8,128)(2,1)}) %reduce-scatter.16.cloned.1.call-update) | async-done | bytes 5406736 | tf_op jit(solution)/shard_map/reduce_scatter | solution.py:38
  1632.7 134.7 %all-gather.5.cloned.1.call-done = bf16[16,440,768]{2,0,1:T(8,128)(2,1)} async-done(((bf16[16,220,768]{2,0,1:T(8,128)(2,1)}), bf16[16,440,768]{2,0,1:T(8,128)(2,1)}) %all-gather.5.cloned.1.call-update) | async-done | bytes 10813456 | tf_op jit(solution)/shard_map/all_gather | solution.py:41
  1767.4 12.4 copy.247
  1779.9 5.8 all-to-all-start.3
  1785.9 192.7 %all-to-all-done.3 = bf16[16,440,768]{2,1,0:T(8,128)(2,1)} async-done(((bf16[16,440,768]{2,1,0:T(8,128)(2,1)}), bf16[16,440,768]{2,1,0:T(8,128)(2,1)}, u32[]{:S(2)}, u32[]{:S(2)}) %all-to-all-start.3) | async-done | bytes 10813472 | tf_op jit(solution)/shard_map/all_to_all | solution.py:42
  1978.6 10.9 convert_reduce_fusion
  1989.5 14.2 gather_fusion.3
  2003.8 6.8 gather.27
  2031.1 5.6 multiply_reduce_fusion.1
  2036.8 4.6 multiply_convert_fusion.2
  2054.7 4.1 copy.293
  2065.8 4.2 reshape.509
  2073.6 5.6 fusion.35
  2079.2 97.6 %all-reduce.19.cloned.1.call-done = bf16[1182,768]{1,0:T(8,128)(2,1)} async-done(((bf16[1182,768]{1,0:T(8,128)(2,1)}), bf16[1182,768]{1,0:T(8,128)(2,1)}) %all-reduce.19.cloned.1.call-update) | async-done | bytes 1815568 | tf_op jit(solution)/shard_map/psum | solution.py:28
  2176.8 4.5 convert_reduce_fusion.4
  2186.2 7.0 fusion.13
  2199.3 57.0 %all-reduce.21.cloned.1.call-done = bf16[1182,768]{1,0:T(8,128)(2,1)} async-done(((bf16[1182,768]{1,0:T(8,128)(2,1)}), bf16[1182,768]{1,0:T(8,128)(2,1)}) %all-reduce.21.cloned.1.call-update) | async-done | bytes 1815568 | tf_op jit(solution)/shard_map/psum | solution.py:28
  2256.2 4.7 convert_reduce_fusion.3
  2278.4 5.6 multiply_reduce_fusion
  2284.1 4.4 multiply_convert_fusion.1
  2301.8 4.2 copy.296
  2313.0 4.2 reshape.512
  2320.9 5.6 fusion.36
  2329.6 6.3 convolution_bitcast_fusion.2
  2348.3 35.2 %all-reduce.23.cloned.1.call-done = bf16[1182,768]{1,0:T(8,128)(2,1)} async-done(((bf16[1182,768]{1,0:T(8,128)(2,1)}), bf16[1182,768]{1,0:T(8,128)(2,1)}) %all-reduce.23.cloned.1.call-update) | async-done | bytes 1815568 | tf_op jit(solution)/shard_map/psum | solution.py:28
  2399.0 13.6 copy.280
  2412.6 5.3 copy.281
  2418.6 8.9 fusion.118
  2427.6 9.7 fusion.70
  2444.6 14.6 convolution_bitcast_fusion.5
  2459.2 14.7 convolution_bitcast_fusion.4
  2473.9 29.6 %all-reduce.1 = f32[768]{0:T(1024)S(1)} all-reduce(f32[768]{0:T(1024)S(1)} %copy-done.118), channel_id=6, replica_groups=mesh['expert'=16,'tensor'=2] {'expert'}, use_global_device_ids=true, to_apply=%region_57.58.clone | all-reduce | flops 768 | bytes 6144
  2504.1 4.7 add_convert_fusion
  2510.2 50.1 %reduce-scatter.22.cloned.1.call-done = f32[48,4]{1,0:T(8,128)} async-done(((f32[768,4]{1,0:T(8,128)}), f32[48,4]{1,0:T(8,128)}) %reduce-scatter.22.cloned.1.call-update) | async-done | bytes 784
  2561.6 186.9 %all-reduce.25.cloned.1.call-done = (f32[2,3,768,384]{3,0,1,2:T(2,128)}, f32[2,384,768]{1,0,2:T(2,128)}) async-done(((f32[2,3,768,384]{3,0,1,2:T(2,128)}, f32[2,384,768]{1,0,2:T(2,128)}), (f32[2,3,768,384]{3,0,1,2:T(2,128)}, f32[2,384,768]{1,0,2:T(2,128)})) %all-reduce.25.cloned.1.call-update) | async-done | bytes 9437200
  2752.1 76.4 %reduce-scatter.18.cloned.1.call-done = f32[48,1536]{1,0:T(8,128)} async-done(((f32[768,1536]{1,0:T(8,128)}), f32[48,1536]{1,0:T(8,128)}) %reduce-scatter.18.cloned.1.call-update) | async-done | bytes 294928 | tf_op jit(solution)/shard_map/reduce_scatter | solution.py:254
  2828.4 79.4 %reduce-scatter.20.cloned.1.call-done = f32[1536,48]{0,1:T(8,128)} async-done(((f32[1536,768]{0,1:T(8,128)}), f32[1536,48]{0,1:T(8,128)}) %reduce-scatter.20.cloned.1.call-update) | async-done | bytes 294928 | tf_op jit(solution)/shard_map/reduce_scatter | solution.py:255
  (503 shorter events, 278.0 us)
Async XLA Ops:
  7.2 120.6 %copy-start = (bf16[1536,768]{1,0:T(8,128)(2,1)S(1)}, bf16[1536,768]{1,0:T(8,128)(2,1)}, u32[]{:S(2)}) copy-start(bf16[1536,768]{1,0:T(8,128)(2,1)} %param.24) | copy-start | bytes 7077892
  7.2 109.7 %all-reduce.13.cloned.1.call-start = ((), (), s32[]{:S(2)}) async-start(), calls=%async_computation.11 | async-start | bytes 3637248 | tf_op jit(solution)/shard_map/psum | solution.py:28
  7.2 6.4 copy-start.3
  10.7 7.2 copy-start.62
  13.6 107.9 %copy-start.104 = (f32[768]{0:T(1024)}, f32[768]{0:T(1024)S(1)}, u32[]{:S(2)}) copy-start(f32[768]{0:T(1024)S(1)} %get-tuple-element.135) | copy-start | bytes 9220
  13.6 286.2 %copy-start.98 = (f32[768]{0:T(1024)}, f32[768]{0:T(1024)S(1)}, u32[]{:S(2)}) copy-start(f32[768]{0:T(1024)S(1)} %get-tuple-element.137) | copy-start | bytes 9220
  57.2 64.3 %copy-start.126 = (f32[768]{0:T(1024)S(1)}, f32[768]{0:T(1024)}, u32[]{:S(2)}) copy-start(f32[768]{0:T(1024)} %get-tuple-element.97) | copy-start | bytes 9220
  57.2 133.0 %all-reduce.15.cloned.1.call-start = ((), (), s32[]{:S(2)}) async-start(), calls=%async_computation.12 | async-start | bytes 3637248 | tf_op jit(solution)/shard_map/psum | solution.py:28
  133.2 163.0 %all-reduce.17.cloned.1.call-start = ((), (), s32[]{:S(2)}) async-start(), calls=%async_computation.13 | async-start | bytes 3637248 | tf_op jit(solution)/shard_map/psum | solution.py:28
  235.3 7.1 copy-start.132
  235.3 7.2 copy-start.115
  235.3 7.2 copy-start.116
  239.2 491.1 %reduce-scatter.14.cloned.1.call-start = ((), (), s32[]{:S(2)}) async-start(), calls=%async_computation.14 | async-start | bytes 16220160 | tf_op jit(solution)/shard_map/reduce_scatter | solution.py:38
  322.3 240.6 %copy-start.140 = (bf16[1,768,768]{2,1,0:T(8,128)(2,1)S(1)}, bf16[1,768,768]{2,1,0:T(8,128)(2,1)}, u32[]{:S(2)}) copy-start(bf16[1,768,768]{2,1,0:T(8,128)(2,1)} %param.26) | copy-start | bytes 3538948
  562.9 20.0 copy-start.138
  605.2 259.7 %all-gather.3.cloned.1.call-start = ((), (), s32[]{:S(2)}) async-start(), calls=%async_computation.15 | async-start | bytes 16220160 | tf_op jit(solution)/shard_map/all_gather | solution.py:41
  876.9 219.3 %copy-start.110 = (bf16[768,8]{0,1:T(8,128)(2,1)S(1)}, bf16[768,8]{0,1:T(8,128)(2,1)}, u32[]{:S(2)}) copy-start(bf16[768,8]{0,1:T(8,128)(2,1)} %param.25) | copy-start | bytes 36868
  876.9 221.3 %copy-start.75 = (s32[1182,2]{0,1:T(2,128)S(1)}, s32[1182,2]{0,1:T(2,128)}, u32[]{:S(2)}) copy-start(s32[1182,2]{0,1:T(2,128)} %param.17) | copy-start | bytes 28372
  876.9 222.2 %all-to-all-start.1 = ((bf16[16,440,768]{2,1,0:T(8,128)(2,1)}), bf16[16,440,768]{2,1,0:T(8,128)(2,1)}, u32[]{:S(2)}, u32[]{:S(2)}) async-start(bf16[16,440,768]{2,1,0:T(8,128)(2,1)} %copy.243), calls=%async_computation.2 | async-start | bytes 21626880 | tf_op jit(solution)/shard_map/all_to_all | solution.py:42
  882.7 750.0 %reduce-scatter.16.cloned.1.call-start = ((), (), s32[]{:S(2)}) async-start(), calls=%async_computation.16 | async-start | bytes 16220160 | tf_op jit(solution)/shard_map/reduce_scatter | solution.py:38
  1096.2 34.9 %copy-start.112 = (pred[2,1182]{1,0:T(4,128)(4,1)}, pred[2,1182]{1,0:T(4,128)(4,1)S(1)}, u32[]{:S(2)}) copy-start(pred[2,1182]{1,0:T(4,128)(4,1)S(1)} %lt.56) | copy-start | bytes 7096
  1098.3 11.8 copy-start.55
  1098.3 11.8 copy-start.60
  1149.4 8.4 copy-start.97
  1178.7 279.8 %copy-start.139 = (bf16[1,768,768]{2,1,0:T(8,128)(2,1)S(1)}, bf16[1,768,768]{2,1,0:T(8,128)(2,1)}, u32[]{:S(2)}) copy-start(bf16[1,768,768]{2,1,0:T(8,128)(2,1)} %param.27) | copy-start | bytes 3538948
  1458.5 28.1 copy-start.31
  1507.7 259.8 %all-gather.5.cloned.1.call-start = ((), (), s32[]{:S(2)}) async-start(), calls=%async_computation.17 | async-start | bytes 16220160 | tf_op jit(solution)/shard_map/all_gather | solution.py:41
  1779.9 198.7 %all-to-all-start.3 = ((bf16[16,440,768]{2,1,0:T(8,128)(2,1)}), bf16[16,440,768]{2,1,0:T(8,128)(2,1)}, u32[]{:S(2)}, u32[]{:S(2)}) async-start(bf16[16,440,768]{2,1,0:T(8,128)(2,1)} %copy.247), calls=%async_computation.5 | async-start | bytes 21626880 | tf_op jit(solution)/shard_map/all_to_all | solution.py:42
  1785.7 391.1 %all-reduce.19.cloned.1.call-start = ((), (), s32[]{:S(2)}) async-start(), calls=%async_computation.18 | async-start | bytes 3637248 | tf_op jit(solution)/shard_map/psum | solution.py:28
  1785.9 228.6 %copy-start.68 = (bf16[1182,8]{0,1:T(8,128)(2,1)}, bf16[1182,8]{0,1:T(8,128)(2,1)S(1)}, u32[]{:S(2)}) copy-start(bf16[1182,8]{0,1:T(8,128)(2,1)S(1)} %select_reduce_fusion.1) | copy-start | bytes 56740
  2003.8 6.8 copy-start.113
  2023.2 8.0 copy-start.35
  2031.1 13.9 slice-start.2
  2036.8 8.2 slice-start.3
  2054.7 8.3 copy-start.40
  2073.6 103.2 %copy-start.67 = (f32[1182]{0:T(1024)S(1)}, f32[1182]{0:T(1024)}, u32[]{:S(2)}) copy-start(f32[1182]{0:T(1024)} %copy-done.66) | copy-start | bytes 14188
  2073.6 103.2 %copy-start.108 = (f32[768]{0:T(1024)S(1)}, f32[768]{0:T(1024)}, u32[]{:S(2)}) copy-start(f32[768]{0:T(1024)} %get-tuple-element.136) | copy-start | bytes 9220
  2079.2 102.2 %copy-start.82 = (f32[1182]{0:T(1024)S(1)}, f32[1182]{0:T(1024)}, u32[]{:S(2)}) copy-start(f32[1182]{0:T(1024)} %copy-done.81) | copy-start | bytes 14188
  2079.2 102.2 %copy-start.95 = (f32[1182]{0:T(1024)S(1)}, f32[1182]{0:T(1024)}, u32[]{:S(2)}) copy-start(f32[1182]{0:T(1024)} %copy-done.94) | copy-start | bytes 14188
  2079.2 177.0 %all-reduce.21.cloned.1.call-start = ((), (), s32[]{:S(2)}) async-start(), calls=%async_computation.19 | async-start | bytes 3637248 | tf_op jit(solution)/shard_map/psum | solution.py:28
  2186.2 7.0 copy-start.29
  2186.2 8.8 copy-start.137
  2195.0 61.2 %copy-start.65 = (f32[1182]{0:T(1024)S(1)}, f32[1182]{0:T(1024)}, u32[]{:S(2)}) copy-start(f32[1182]{0:T(1024)} %copy-done.64) | copy-start | bytes 14188
  2195.0 61.2 %copy-start.105 = (f32[768]{0:T(1024)S(1)}, f32[768]{0:T(1024)}, u32[]{:S(2)}) copy-start(f32[768]{0:T(1024)} %copy-done.104) | copy-start | bytes 9220
  2199.2 61.8 %copy-start.80 = (f32[1182]{0:T(1024)S(1)}, f32[1182]{0:T(1024)}, u32[]{:S(2)}) copy-start(f32[1182]{0:T(1024)} %copy-done.79) | copy-start | bytes 14188
  2199.2 61.8 %copy-start.92 = (f32[1182]{0:T(1024)S(1)}, f32[1182]{0:T(1024)}, u32[]{:S(2)}) copy-start(f32[1182]{0:T(1024)} %copy-done.91) | copy-start | bytes 14188
  2199.2 184.3 %all-reduce.23.cloned.1.call-start = ((), (), s32[]{:S(2)}) async-start(), calls=%async_computation.20 | async-start | bytes 3637248 | tf_op jit(solution)/shard_map/psum | solution.py:28
  2270.4 8.0 copy-start.33
  2278.4 13.7 slice-start
  2284.1 8.0 slice-start.1
  2301.8 8.3 copy-start.41
  2326.5 116.7 %reduce-scatter.26.cloned.1.call-start = ((), (), s32[]{:S(2)}) async-start(), calls=%async_computation.25 | async-start | bytes 417792
  2329.5 179.3 %reduce-scatter.24.cloned.1.call-start = ((), (), s32[]{:S(2)}) async-start(), calls=%async_computation.24 | async-start | bytes 417792
  2383.5 6.7 copy-start.124
  2383.5 6.7 copy-start.125
  2393.0 167.2 %reduce-scatter.22.cloned.1.call-start = ((), (), s32[]{:S(2)}) async-start(), calls=%async_computation.23 | async-start | bytes 417792
  2396.1 352.4 %all-reduce.25.cloned.1.call-start = ((), (), s32[]{:S(2)}) async-start(), calls=%async_computation.26 | async-start | bytes 18874368
  2418.0 410.5 %reduce-scatter.18.cloned.1.call-start = ((), (), s32[]{:S(2)}) async-start(), calls=%async_computation.21 | async-start | bytes 5013504 | tf_op jit(solution)/shard_map/reduce_scatter | solution.py:254
  2427.5 480.3 %reduce-scatter.20.cloned.1.call-start = ((), (), s32[]{:S(2)}) async-start(), calls=%async_computation.22 | async-start | bytes 5013504 | tf_op jit(solution)/shard_map/reduce_scatter | solution.py:255
  2459.2 14.7 copy-start.118
  2459.2 44.9 %copy-start.114 = (f32[1182]{0:T(1024)S(1)}, f32[1182]{0:T(1024)}, u32[]{:S(2)}) copy-start(f32[1182]{0:T(1024)} %get-tuple-element.79) | copy-start | bytes 14188
  2459.2 44.9 %copy-start.86 = (f32[1182]{0:T(1024)S(1)}, f32[1182]{0:T(1024)}, u32[]{:S(2)}) copy-start(f32[1182]{0:T(1024)} %copy-done.85) | copy-start | bytes 14188
  2459.2 44.9 %copy-start.90 = (f32[1182]{0:T(1024)S(1)}, f32[1182]{0:T(1024)}, u32[]{:S(2)}) copy-start(f32[1182]{0:T(1024)} %copy-done.87) | copy-start | bytes 14188
  2459.2 44.9 %copy-start.103 = (f32[768]{0:T(1024)S(1)}, f32[768]{0:T(1024)}, u32[]{:S(2)}) copy-start(f32[768]{0:T(1024)} %copy-done.100) | copy-start | bytes 9220
  (105 other events, 345.3 us)
Sparse Core Ops, SparseCore 0:
  57.3 59.5 all-reduce.12
  133.3 56.8 all-reduce.14
  239.3 56.8 all-reduce.16
  605.3 124.8 reduce-scatter.13
  731.7 133.0 all-gather.2
  1507.8 124.8 reduce-scatter.15
  1634.2 133.1 all-gather.4
  2079.3 97.4 all-reduce.18
  2199.3 56.8 all-reduce.20
  2326.6 56.8 all-reduce.22
  2387.6 55.5 reduce-scatter.25
  2446.9 54.6 reduce-scatter.23
  2505.7 54.5 reduce-scatter.21
  2564.3 184.1 all-reduce.24
  2752.8 75.6 reduce-scatter.17
  2833.2 74.5 reduce-scatter.19
where the time goes:
time: 2920 us; the launch traced here: 2910 us
  waiting for transfers between devices  1450 us (50%)
  blocking collectives  761 us (26%)
  local copies, waits for them, and re-layouts  324 us (11%)
  matrix products  221 us (8%)
  other arithmetic  123 us (4%)
    all_to_all x2, blocking collectives, to_experts(): lax.all_to_all(doubled, 'expert', split_axis=0, concat_axis=0, tiled=True)  520 us
    psum x6, waiting for transfers between devices, tensor_total(): lax.psum(partial_value.astype(jnp.bfloat16), 'tensor').astype(jnp.float32)  346 us
    all_gather x2, waiting for transfers between devices, from_experts(): full_rows = lax.all_gather(share_rows, 'tensor', axis=1, tiled=True)  269 us
    reduce_scatter x2, waiting for transfers between devices, from_experts(): lax.psum_scatter(partial_value.astype(jnp.bfloat16), 'tensor', scatter_di...  250 us
    unnamed x20, waiting for transfers between devices  241 us
    psum x1, blocking collectives, body(): valid_count = lax.psum(local_count, 'expert')  211 us
    all_to_all x2, waiting for transfers between devices, from_experts(): lax.all_to_all(full_rows, 'expert', split_axis=0, concat_axis=0, tiled=True)  193 us
    reduce_scatter x1, waiting for transfers between devices, body(): lax.psum_scatter(grad_mlp_out, 'expert', scatter_dimension=1, tiled=True)  79.4 us
  transfers between devices with their start and end apart: 18, of which 16 were waited for; matrix products, arithmetic and copies ran while one was open for 5% of the time, Pallas kernels for 0%

commit v1 on v0

--- a/solution.py
+++ b/solution.py
@@ -39,7 +39,15 @@
         partial_value.astype(jnp.bfloat16), "tensor", scatter_dimension=1, tiled=True
     )
     full_rows = lax.all_gather(share_rows, "tensor", axis=1, tiled=True)
-    back_rows = lax.all_to_all(full_rows, "expert", split_axis=0, concat_axis=0, tiled=True)
+    ways, here = (lax.axis_size("expert"), lax.axis_index("expert"))
+    width = full_rows.shape[0] // ways
+    turned = jnp.roll(full_rows, -here * width, axis=0)
+    got = [lax.slice_in_dim(turned, 0, width, axis=0)]
+    for far in range(1, ways):
+        sent = lax.slice_in_dim(turned, far * width, (far + 1) * width, axis=0)
+        got.append(lax.ppermute(sent, "expert", [(d, (d + far) % ways) for d in range(ways)]))
+    line = jnp.concatenate(got[::-1], axis=0)
+    back_rows = jnp.roll(line, (here + 1) * got[0].shape[0], axis=0)
     slots_each = back_rows.shape[1]
     halves = back_rows.reshape(experts, 2, slots_each, -1).astype(jnp.float32)
     return jnp.sum(halves, axis=1).reshape(experts * slots_each, -1)

time: 2920 us -> 3470 us (1.19)
  local copies, waits for them, and re-layouts: 324 us -> 674 us
  other arithmetic: 123 us -> 327 us
  blocking collectives: 761 us -> 642 us
  starting transfers between devices: 12.7 us -> 99.5 us
    ppermute x0 -> x30, waiting for transfers between devices: none -> 245 us  [from_experts(): lax.ppermute(sent, 'expert', [(d, (d + far) % ways) for d in range(ways)])]
    all_to_all x2 -> x0, waiting for transfers between devices: 193 us -> none  [from_experts(): lax.all_to_all(full_rows, 'expert', split_axis=0, concat_axis=0, tiled=True)]
    reduce_sum x2, other arithmetic: 21.9 us -> 173 us  [from_experts(): return jnp.sum(halves, axis=1).reshape(experts * slots_each, -1)]
    concatenate x0 -> x2, local copies, waits for them, and re-layouts: none -> 116 us  [from_experts(): line = jnp.concatenate(got[::-1], axis=0)]
    ppermute x0 -> x30, starting transfers between devices: none -> 98.3 us  [from_experts(): lax.ppermute(sent, 'expert', [(d, (d + far) % ways) for d in range(ways)])]
    slice x1 -> x33, local copies, waits for them, and re-layouts: 0.3 us -> 98.5 us  [the longest x2 73 us: from_experts(): got = [lax.slice_in_dim(turned, 0, width, axis=0)]]
    ppermute x0 -> x30, local copies, waits for them, and re-layouts: none -> 89.5 us  [from_experts(): lax.ppermute(sent, 'expert', [(d, (d + far) % ways) for d in range(ways)])]
    psum x1, blocking collectives: 211 us -> 134 us  [body(): valid_count = lax.psum(local_count, 'expert')]
  transfers between devices with their start and end apart: 18 -> 46, of which waited for: 16 -> 29; matrix products, arithmetic and copies ran while one was open for 5% -> 7% of each run, Pallas kernels for 0% -> 0%
where the time goes in v1:
time: 3470 us; the launch traced here: 3450 us
  waiting for transfers between devices  1460 us (42%)
  local copies, waits for them, and re-layouts  674 us (19%)
  blocking collectives  642 us (19%)
  other arithmetic  327 us (9%)
  matrix products  224 us (6%)
  starting transfers between devices  99.5 us (3%)
    all_to_all x2, blocking collectives, to_experts(): lax.all_to_all(doubled, 'expert', split_axis=0, concat_axis=0, tiled=True)  479 us
    psum x6, waiting for transfers between devices, tensor_total(): lax.psum(partial_value.astype(jnp.bfloat16), 'tensor').astype(jnp.float32)  304 us
    all_gather x2, waiting for transfers between devices, from_experts(): full_rows = lax.all_gather(share_rows, 'tensor', axis=1, tiled=True)  269 us
    reduce_scatter x2, waiting for transfers between devices, from_experts(): lax.psum_scatter(partial_value.astype(jnp.bfloat16), 'tensor', scatter_di...  249 us
    ppermute x30, waiting for transfers between devices, from_experts(): lax.ppermute(sent, 'expert', [(d, (d + far) % ways) for d in range(ways)])  245 us
    unnamed x20, waiting for transfers between devices  241 us
    reduce_sum x2, other arithmetic, from_experts(): return jnp.sum(halves, axis=1).reshape(experts * slots_each, -1)  173 us
    psum x1, blocking collectives, body(): valid_count = lax.psum(local_count, 'expert')  134 us
  transfers between devices with their start and end apart: 46, of which 29 were waited for; matrix products, arithmetic and copies ran while one was open for 7% of the time, Pallas kernels for 0%

profile of v1, /device:TPU:0, one launch (start us, length us, event | category | flops | bytes accessed | tf_op | source)
XLA Modules:
  0.0 3448.8 jit_solution(12692426500911778415)
XLA Ops:
  56.1 59.5 %all-reduce.13.cloned.1.call-done = bf16[1182,768]{1,0:T(8,128)(2,1)} async-done(((bf16[1182,768]{1,0:T(8,128)(2,1)}), bf16[1182,768]{1,0:T(8,128)(2,1)}) %all-reduce.13.cloned.1.call-update) | async-done | bytes 1815568 | tf_op jit(solution)/shard_map/psum | solution.py:28
  132.6 56.3 %all-reduce.15.cloned.1.call-done = bf16[1182,768]{1,0:T(8,128)(2,1)} async-done(((bf16[1182,768]{1,0:T(8,128)(2,1)}), bf16[1182,768]{1,0:T(8,128)(2,1)}) %all-reduce.15.cloned.1.call-update) | async-done | bytes 1815568 | tf_op jit(solution)/shard_map/psum | solution.py:28
  241.1 12.7 scatter_custom_fusion
  254.6 40.2 %all-reduce.17.cloned.1.call-done = bf16[1182,768]{1,0:T(8,128)(2,1)} async-done(((bf16[1182,768]{1,0:T(8,128)(2,1)}), bf16[1182,768]{1,0:T(8,128)(2,1)}) %all-reduce.17.cloned.1.call-update) | async-done | bytes 1815568 | tf_op jit(solution)/shard_map/psum | solution.py:28
  300.9 15.7 gather_fusion
  321.0 240.6 %all_to_all.10 = bf16[16,440,768]{2,1,0:T(8,128)(2,1)} all-to-all(bf16[16,440,768]{2,1,0:T(8,128)(2,1)S(1)} %bitcast.187), channel_id=1, replica_groups=mesh['expert'=16,'tensor'=2] {'expert'}, dimensions={0} | all-to-all | bytes 21626880 | tf_op jit(solution)/shard_map/all_to_all | solution.py:33
  561.5 20.1 multiply_convert_fusion
  581.6 13.2 convolution_convert_fusion.1
  594.8 9.1 copy.298
  603.9 125.0 %reduce-scatter.14.cloned.1.call-done = bf16[16,220,768]{2,0,1:T(8,128)(2,1)} async-done(((bf16[16,440,768]{2,0,1:T(8,128)(2,1)}), bf16[16,220,768]{2,0,1:T(8,128)(2,1)}) %reduce-scatter.14.cloned.1.call-update) | async-done | bytes 5406736 | tf_op jit(solution)/shard_map/reduce_scatter | solution.py:38
  729.2 134.4 %all-gather.3.cloned.1.call-done = bf16[16,440,768]{2,0,1:T(8,128)(2,1)} async-done(((bf16[16,220,768]{2,0,1:T(8,128)(2,1)}), bf16[16,440,768]{2,0,1:T(8,128)(2,1)}) %all-gather.3.cloned.1.call-update) | async-done | bytes 10813456 | tf_op jit(solution)/shard_map/all_gather | solution.py:41
  863.6 12.6 fusion.12
  876.2 36.2 %fusion.130 = (bf16[1,440,768]{2,0,1:T(2,128)(2,1)}, bf16[1,440,768]{2,0,1:T(2,128)(2,1)}, bf16[1,440,768]{2,0,1:T(2,128)(2,1)}, bf16[1,440,768]{2,0,1:T(2,128)(...) fusion(bf16[16,440,768]{2,0,1:T(8,128)(2,1)} %fusion.12), kind=kLoop, calls=%fused_computation.282 | loop fusion | bytes 21626880 | tf_op jit(solution)/shard_map/slice | solution.py:45
  927.3 9.0 collective-permute-done
  936.3 14.5 collective-permute-done.1
  950.8 14.5 collective-permute-done.2
  965.3 14.5 collective-permute-done.3
  979.8 14.5 collective-permute-done.4
  995.5 133.6 %psum.52 = f32[]{:T(128)} all-reduce(f32[]{:T(128)S(6)} %mul_shard_map.3), channel_id=1, replica_groups=mesh['expert'=16,'tensor'=2] {'expert'}, use_global_device_ids=true, to_apply=%region_27.29 | all-reduce | flops 1 | bytes 8 | tf_op jit(solution)/shard_map/psum | solution.py:155
  1180.0 36.1 %collective-permute-done.10 = bf16[1,440,768]{2,1,0:T(8,128)(2,1)} collective-permute-done((bf16[1,440,768]{2,1,0:T(8,128)(2,1)}, bf16[1,440,768]{2,1,0:T(8,128)(2,1)}, u32[]{:S(2)}, u32[]{:S(2)}) %collective-permute-start.10) | collective-permute-done | bytes 675872 | tf_op jit(solution)/shard_map/ppermute | solution.py:48
  1232.4 57.8 %concatenate.31 = bf16[16,440,768]{2,0,1:T(8,128)(2,1)} concatenate(bf16[1,440,768]{2,0,1:T(2,128)(2,1)} %copy.314, bf16[1,440,768]{2,0,1:T(2,128)(2,1)} %copy.315, bf16[1,440,768]{2,0,1:T(2,128)(2,1)} %copy.316, bf16[1,440,768]{2,0,1:T(2,128)(2,1)} %copy.317, bf16[1,440,768]{2,0,1:T(2,128)(2,1)} %copy.318, bf16[1,440,768]{2,0,1:T(2,128)(2,1)} %copy.319, ...), dimensions={0} | concatenate | bytes 21626880 | tf_op jit(solution)/shard_map/concatenate | solution.py:49
  1290.2 16.9 fusion.11
  1307.1 25.2 reshape.457
  1332.3 86.4 %reduce_sum.387 = f32[8,440,768]{2,0,1:T(8,128)} reduce(f32[8,2,440,768]{3,1,0,2:T(2,128)} %reshape.457, f32[]{:T(128)} %constant.48.clone.1), dimensions={1}, to_apply=%region_24.26 | reduce | flops 2703360 | bytes 32440324 | tf_op jit(solution)/shard_map/reduce_sum | solution.py:53
  1418.7 11.6 copy.329
  1430.4 14.5 gather_fusion.1
  1470.0 8.4 multiply_reduce_fusion.2
  1478.4 16.4 gather_fusion.2
  1499.3 238.1 %all_to_all.11 = bf16[16,440,768]{2,1,0:T(8,128)(2,1)S(1)} all-to-all(bf16[16,440,768]{2,1,0:T(8,128)(2,1)S(1)} %bitcast.188), channel_id=1, replica_groups=mesh['expert'=16,'tensor'=2] {'expert'}, dimensions={0} | all-to-all | bytes 21626880 | tf_op jit(solution)/shard_map/all_to_all | solution.py:33
  1737.4 28.2 fusion.6
  1765.5 13.3 convolution_convert_fusion
  1778.8 9.1 copy.330
  1788.0 124.3 %reduce-scatter.16.cloned.1.call-done = bf16[16,220,768]{2,0,1:T(8,128)(2,1)} async-done(((bf16[16,440,768]{2,0,1:T(8,128)(2,1)}), bf16[16,220,768]{2,0,1:T(8,128)(2,1)}) %reduce-scatter.16.cloned.1.call-update) | async-done | bytes 5406736 | tf_op jit(solution)/shard_map/reduce_scatter | solution.py:38
  1912.3 134.6 %all-gather.5.cloned.1.call-done = bf16[16,440,768]{2,0,1:T(8,128)(2,1)} async-done(((bf16[16,220,768]{2,0,1:T(8,128)(2,1)}), bf16[16,440,768]{2,0,1:T(8,128)(2,1)}) %all-gather.5.cloned.1.call-update) | async-done | bytes 10813456 | tf_op jit(solution)/shard_map/all_gather | solution.py:41
  2047.0 12.8 fusion.9
  2059.8 36.8 %fusion.129 = (bf16[1,440,768]{2,0,1:T(2,128)(2,1)}, bf16[1,440,768]{2,0,1:T(2,128)(2,1)}, bf16[1,440,768]{2,0,1:T(2,128)(2,1)}, bf16[1,440,768]{2,0,1:T(2,128)(...) fusion(bf16[16,440,768]{2,0,1:T(8,128)(2,1)} %fusion.9), kind=kLoop, calls=%fused_computation.281 | loop fusion | bytes 21626880 | tf_op jit(solution)/shard_map/slice | solution.py:45
  2111.6 8.9 collective-permute-done.15
  2120.5 14.5 collective-permute-done.16
  2135.0 14.5 collective-permute-done.17
  2149.4 14.5 collective-permute-done.18
  2163.9 14.5 collective-permute-done.19
  2181.9 11.1 collective-permute-done.20
  2193.0 44.8 %collective-permute-start.25 = (bf16[1,440,768]{2,1,0:T(8,128)(2,1)S(1)}, bf16[1,440,768]{2,1,0:T(8,128)(2,1)S(1)}, u32[]{:S(2)}, u32[]{:S(2)}) collective-permute-start(bf16[1,440,768]{2,1,0:T(8,128)(2,1)S(1)} %copy.341), channel_id=1, source_target_pairs={{0,10},{2,12},{4,14},{6,16},{8,18},{10,20},{12,22},{14,24},{16,26}... | collective-permute-start | bytes 2027528 | tf_op jit(solution)/shard_map/ppermute | solution.py:48
  2237.8 29.1 collective-permute-start.26
  2266.9 63.7 %collective-permute-done.22 = bf16[1,440,768]{2,1,0:T(8,128)(2,1)} collective-permute-done((bf16[1,440,768]{2,1,0:T(8,128)(2,1)}, bf16[1,440,768]{2,1,0:T(8,128)(2,1)}, u32[]{:S(2)}, u32[]{:S(2)}) %collective-permute-start.22) | collective-permute-done | bytes 675872 | tf_op jit(solution)/shard_map/ppermute | solution.py:48
  2373.3 57.8 %concatenate.32 = bf16[16,440,768]{2,0,1:T(8,128)(2,1)} concatenate(bf16[1,440,768]{2,0,1:T(2,128)(2,1)} %copy.346, bf16[1,440,768]{2,0,1:T(2,128)(2,1)} %copy.347, bf16[1,440,768]{2,0,1:T(2,128)(2,1)} %copy.348, bf16[1,440,768]{2,0,1:T(2,128)(2,1)} %copy.349, bf16[1,440,768]{2,0,1:T(2,128)(2,1)} %copy.350, bf16[1,440,768]{2,0,1:T(2,128)(2,1)} %copy.351, ...), dimensions={0} | concatenate | bytes 21626880 | tf_op jit(solution)/shard_map/concatenate | solution.py:49
  2431.1 16.9 fusion.8
  2448.0 25.3 reshape.458
  2473.3 86.6 %reduce_sum.393 = f32[8,440,768]{2,0,1:T(8,128)} reduce(f32[8,2,440,768]{3,1,0,2:T(2,128)} %reshape.458, f32[]{:T(128)} %constant.48.clone.1), dimensions={1}, to_apply=%region_29.31 | reduce | flops 2703360 | bytes 32440324 | tf_op jit(solution)/shard_map/reduce_sum | solution.py:53
  2559.8 11.5 copy.361
  2571.4 14.6 gather_fusion.3
  2657.6 57.5 %all-reduce.19.cloned.1.call-done = bf16[1182,768]{1,0:T(8,128)(2,1)} async-done(((bf16[1182,768]{1,0:T(8,128)(2,1)}), bf16[1182,768]{1,0:T(8,128)(2,1)}) %all-reduce.19.cloned.1.call-update) | async-done | bytes 1815568 | tf_op jit(solution)/shard_map/psum | solution.py:28
  2737.5 57.0 %all-reduce.21.cloned.1.call-done = bf16[1182,768]{1,0:T(8,128)(2,1)} async-done(((bf16[1182,768]{1,0:T(8,128)(2,1)}), bf16[1182,768]{1,0:T(8,128)(2,1)}) %all-reduce.21.cloned.1.call-update) | async-done | bytes 1815568 | tf_op jit(solution)/shard_map/psum | solution.py:28
  2883.9 33.6 all-reduce.23.cloned.1.call-done
  2938.4 13.6 copy.392
  2952.3 9.7 fusion.76
  2962.7 8.9 fusion.124
  2978.6 14.6 convolution_bitcast_fusion.4
  2993.2 14.7 convolution_bitcast_fusion.5
  3007.9 29.6 all-reduce.1
  3044.2 50.1 %reduce-scatter.22.cloned.1.call-done = f32[48,4]{1,0:T(8,128)} async-done(((f32[768,4]{1,0:T(8,128)}), f32[48,4]{1,0:T(8,128)}) %reduce-scatter.22.cloned.1.call-update) | async-done | bytes 784
  3095.7 186.8 %all-reduce.25.cloned.1.call-done = (f32[2,3,768,384]{3,0,1,2:T(2,128)}, f32[2,384,768]{1,0,2:T(2,128)}) async-done(((f32[2,3,768,384]{3,0,1,2:T(2,128)}, f32[2,384,768]{1,0,2:T(2,128)}), (f32[2,3,768,384]{3,0,1,2:T(2,128)}, f32[2,384,768]{1,0,2:T(2,128)})) %all-reduce.25.cloned.1.call-update) | async-done | bytes 9437200
  3286.1 76.4 %reduce-scatter.20.cloned.1.call-done = f32[1536,48]{0,1:T(8,128)} async-done(((f32[1536,768]{0,1:T(8,128)}), f32[1536,48]{0,1:T(8,128)}) %reduce-scatter.20.cloned.1.call-update) | async-done | bytes 294928 | tf_op jit(solution)/shard_map/reduce_scatter | solution.py:263
  3362.5 79.4 %reduce-scatter.18.cloned.1.call-done = f32[48,1536]{1,0:T(8,128)} async-done(((f32[768,1536]{1,0:T(8,128)}), f32[48,1536]{1,0:T(8,128)}) %reduce-scatter.18.cloned.1.call-update) | async-done | bytes 294928 | tf_op jit(solution)/shard_map/reduce_scatter | solution.py:262
  (657 shorter events, 523.6 us)
Async XLA Ops:
  7.2 119.3 %copy-start = (bf16[1536,768]{1,0:T(8,128)(2,1)S(1)}, bf16[1536,768]{1,0:T(8,128)(2,1)}, u32[]{:S(2)}) copy-start(bf16[1536,768]{1,0:T(8,128)(2,1)} %param.26) | copy-start | bytes 7077892
  7.2 108.3 %all-reduce.13.cloned.1.call-start = ((), (), s32[]{:S(2)}) async-start(), calls=%async_computation.9 | async-start | bytes 3637248 | tf_op jit(solution)/shard_map/psum | solution.py:28
  12.2 108.0 %copy-start.115 = (f32[768]{0:T(1024)}, f32[768]{0:T(1024)S(1)}, u32[]{:S(2)}) copy-start(f32[768]{0:T(1024)S(1)} %get-tuple-element.168) | copy-start | bytes 9220
  12.2 286.2 %copy-start.109 = (f32[768]{0:T(1024)}, f32[768]{0:T(1024)S(1)}, u32[]{:S(2)}) copy-start(f32[768]{0:T(1024)S(1)} %get-tuple-element.170) | copy-start | bytes 9220
  55.9 64.3 %copy-start.140 = (f32[768]{0:T(1024)S(1)}, f32[768]{0:T(1024)}, u32[]{:S(2)}) copy-start(f32[768]{0:T(1024)} %get-tuple-element.98) | copy-start | bytes 9220
  55.9 133.0 %all-reduce.15.cloned.1.call-start = ((), (), s32[]{:S(2)}) async-start(), calls=%async_computation.10 | async-start | bytes 3637248 | tf_op jit(solution)/shard_map/psum | solution.py:28
  131.9 162.9 %all-reduce.17.cloned.1.call-start = ((), (), s32[]{:S(2)}) async-start(), calls=%async_computation.11 | async-start | bytes 3637248 | tf_op jit(solution)/shard_map/psum | solution.py:28
  237.8 491.2 %reduce-scatter.14.cloned.1.call-start = ((), (), s32[]{:S(2)}) async-start(), calls=%async_computation.12 | async-start | bytes 16220160 | tf_op jit(solution)/shard_map/reduce_scatter | solution.py:38
  253.9 62.6 %copy-start.124 = (pred[8,440]{1,0:T(8,128)(4,1)}, pred[8,440]{1,0:T(8,128)(4,1)S(1)}, u32[]{:S(2)}) copy-start(pred[8,440]{1,0:T(8,128)(4,1)S(1)} %broadcast_in_dim.159) | copy-start | bytes 10564
  320.9 240.6 %copy-start.153 = (bf16[1,768,768]{2,1,0:T(8,128)(2,1)S(1)}, bf16[1,768,768]{2,1,0:T(8,128)(2,1)}, u32[]{:S(2)}) copy-start(bf16[1,768,768]{2,1,0:T(8,128)(2,1)} %param.28) | copy-start | bytes 3538948
  603.9 259.7 %all-gather.3.cloned.1.call-start = ((), (), s32[]{:S(2)}) async-start(), calls=%async_computation.13 | async-start | bytes 16220160 | tf_op jit(solution)/shard_map/all_gather | solution.py:41
  729.0 1183.3 %reduce-scatter.16.cloned.1.call-start = ((), (), s32[]{:S(2)}) async-start(), calls=%async_computation.14 | async-start | bytes 16220160 | tf_op jit(solution)/shard_map/reduce_scatter | solution.py:38
  915.6 20.8 collective-permute-start
  920.8 30.0 collective-permute-start.1
  921.5 43.8 %collective-permute-start.2 = (bf16[1,440,768]{2,1,0:T(8,128)(2,1)S(1)}, bf16[1,440,768]{2,1,0:T(8,128)(2,1)}, u32[]{:S(2)}, u32[]{:S(2)}) collective-permute-start(bf16[1,440,768]{2,1,0:T(8,128)(2,1)S(1)} %copy.301), channel_id=1, source_target_pairs={{0,26},{2,28},{4,30},{6,0},{8,2},{10,4},{12,6},{14,8},{16,10},{18,... | collective-permute-start | bytes 2027528 | tf_op jit(solution)/shard_map/ppermute | solution.py:48
  921.9 57.9 %collective-permute-start.3 = (bf16[1,440,768]{2,1,0:T(8,128)(2,1)S(1)}, bf16[1,440,768]{2,1,0:T(8,128)(2,1)}, u32[]{:S(2)}, u32[]{:S(2)}) collective-permute-start(bf16[1,440,768]{2,1,0:T(8,128)(2,1)S(1)} %copy.302), channel_id=1, source_target_pairs={{0,24},{2,26},{4,28},{6,30},{8,0},{10,2},{12,4},{14,6},{16,8},{18,... | collective-permute-start | bytes 2027528 | tf_op jit(solution)/shard_map/ppermute | solution.py:48
  922.4 71.9 %collective-permute-start.4 = (bf16[1,440,768]{2,1,0:T(8,128)(2,1)S(1)}, bf16[1,440,768]{2,1,0:T(8,128)(2,1)}, u32[]{:S(2)}, u32[]{:S(2)}) collective-permute-start(bf16[1,440,768]{2,1,0:T(8,128)(2,1)S(1)} %copy.303), channel_id=1, source_target_pairs={{0,22},{2,24},{4,26},{6,28},{8,30},{10,0},{12,2},{14,4},{16,6},{18... | collective-permute-start | bytes 2027528 | tf_op jit(solution)/shard_map/ppermute | solution.py:48
  923.6 70.7 %copy-start.155 = (s32[6]{0:T(128)S(1)}, s32[6]{0:T(128)}, u32[]{:S(2)}) copy-start(s32[6]{0:T(128)} %param.18) | copy-start | bytes 76
  923.6 206.6 %copy-start.120 = (bf16[768,8]{0,1:T(8,128)(2,1)S(1)}, bf16[768,8]{0,1:T(8,128)(2,1)}, u32[]{:S(2)}) copy-start(bf16[768,8]{0,1:T(8,128)(2,1)} %param.27) | copy-start | bytes 36868
  936.3 202.2 %collective-permute-start.5 = (bf16[1,440,768]{2,1,0:T(8,128)(2,1)}, bf16[1,440,768]{2,1,0:T(8,128)(2,1)}, u32[]{:S(2)}, u32[]{:S(2)}) collective-permute-start(bf16[1,440,768]{2,1,0:T(8,128)(2,1)} %copy.304), channel_id=1, source_target_pairs={{0,20},{2,22},{4,24},{6,26},{8,28},{10,30},{12,0},{14,2},{16,4},{1... | collective-permute-start | bytes 2027528 | tf_op jit(solution)/shard_map/ppermute | solution.py:48
  950.8 191.4 %collective-permute-start.6 = (bf16[1,440,768]{2,1,0:T(8,128)(2,1)}, bf16[1,440,768]{2,1,0:T(8,128)(2,1)}, u32[]{:S(2)}, u32[]{:S(2)}) collective-permute-start(bf16[1,440,768]{2,1,0:T(8,128)(2,1)} %copy.305), channel_id=1, source_target_pairs={{0,18},{2,20},{4,22},{6,24},{8,26},{10,28},{12,30},{14,0},{16,2},{... | collective-permute-start | bytes 2027528 | tf_op jit(solution)/shard_map/ppermute | solution.py:48
  965.3 178.3 %collective-permute-start.7 = (bf16[1,440,768]{2,1,0:T(8,128)(2,1)}, bf16[1,440,768]{2,1,0:T(8,128)(2,1)}, u32[]{:S(2)}, u32[]{:S(2)}) collective-permute-start(bf16[1,440,768]{2,1,0:T(8,128)(2,1)} %copy.306), channel_id=1, source_target_pairs={{0,16},{2,18},{4,20},{6,22},{8,24},{10,26},{12,28},{14,30},{16,0},... | collective-permute-start | bytes 2027528 | tf_op jit(solution)/shard_map/ppermute | solution.py:48
  979.8 168.2 %collective-permute-start.8 = (bf16[1,440,768]{2,1,0:T(8,128)(2,1)}, bf16[1,440,768]{2,1,0:T(8,128)(2,1)}, u32[]{:S(2)}, u32[]{:S(2)}) collective-permute-start(bf16[1,440,768]{2,1,0:T(8,128)(2,1)} %copy.307), channel_id=1, source_target_pairs={{0,14},{2,16},{4,18},{6,20},{8,22},{10,24},{12,26},{14,28},{16,30}... | collective-permute-start | bytes 2027528 | tf_op jit(solution)/shard_map/ppermute | solution.py:48
  994.3 153.8 %collective-permute-start.9 = (bf16[1,440,768]{2,1,0:T(8,128)(2,1)}, bf16[1,440,768]{2,1,0:T(8,128)(2,1)}, u32[]{:S(2)}, u32[]{:S(2)}) collective-permute-start(bf16[1,440,768]{2,1,0:T(8,128)(2,1)} %copy.308), channel_id=1, source_target_pairs={{0,12},{2,14},{4,16},{6,18},{8,20},{10,22},{12,24},{14,26},{16,28}... | collective-permute-start | bytes 2027528 | tf_op jit(solution)/shard_map/ppermute | solution.py:48
  1130.1 321.4 %copy-start.122 = (pred[2,1182]{1,0:T(4,128)(4,1)}, pred[2,1182]{1,0:T(4,128)(4,1)S(1)}, u32[]{:S(2)}) copy-start(pred[2,1182]{1,0:T(4,128)(4,1)S(1)} %lt.65) | copy-start | bytes 7096
  1130.2 300.2 %copy-start.84 = (s32[3072]{0:T(1024)}, s32[3072]{0:T(1024)S(1)}, u32[]{:S(2)}) copy-start(s32[3072]{0:T(1024)S(1)} %pad_clamp_fusion.2) | copy-start | bytes 36868
  1138.6 77.5 %collective-permute-start.10 = (bf16[1,440,768]{2,1,0:T(8,128)(2,1)}, bf16[1,440,768]{2,1,0:T(8,128)(2,1)}, u32[]{:S(2)}, u32[]{:S(2)}) collective-permute-start(bf16[1,440,768]{2,1,0:T(8,128)(2,1)} %copy.309), channel_id=1, source_target_pairs={{0,10},{2,12},{4,14},{6,16},{8,18},{10,20},{12,22},{14,24},{16,26}... | collective-permute-start | bytes 2027528 | tf_op jit(solution)/shard_map/ppermute | solution.py:48
  1142.2 77.3 %collective-permute-start.11 = (bf16[1,440,768]{2,1,0:T(8,128)(2,1)}, bf16[1,440,768]{2,1,0:T(8,128)(2,1)}, u32[]{:S(2)}, u32[]{:S(2)}) collective-permute-start(bf16[1,440,768]{2,1,0:T(8,128)(2,1)} %copy.310), channel_id=1, source_target_pairs={{0,8},{2,10},{4,12},{6,14},{8,16},{10,18},{12,20},{14,22},{16,24},... | collective-permute-start | bytes 2027528 | tf_op jit(solution)/shard_map/ppermute | solution.py:48
  1143.6 79.0 %collective-permute-start.12 = (bf16[1,440,768]{2,1,0:T(8,128)(2,1)}, bf16[1,440,768]{2,1,0:T(8,128)(2,1)}, u32[]{:S(2)}, u32[]{:S(2)}) collective-permute-start(bf16[1,440,768]{2,1,0:T(8,128)(2,1)} %copy.311), channel_id=1, source_target_pairs={{0,6},{2,8},{4,10},{6,12},{8,14},{10,16},{12,18},{14,20},{16,22},{... | collective-permute-start | bytes 2027528 | tf_op jit(solution)/shard_map/ppermute | solution.py:48
  1148.0 77.9 %collective-permute-start.13 = (bf16[1,440,768]{2,1,0:T(8,128)(2,1)}, bf16[1,440,768]{2,1,0:T(8,128)(2,1)}, u32[]{:S(2)}, u32[]{:S(2)}) collective-permute-start(bf16[1,440,768]{2,1,0:T(8,128)(2,1)} %copy.312), channel_id=1, source_target_pairs={{0,4},{2,6},{4,8},{6,10},{8,12},{10,14},{12,16},{14,18},{16,20},{1... | collective-permute-start | bytes 2027528 | tf_op jit(solution)/shard_map/ppermute | solution.py:48
  1148.0 81.2 %collective-permute-start.14 = (bf16[1,440,768]{2,1,0:T(8,128)(2,1)}, bf16[1,440,768]{2,1,0:T(8,128)(2,1)}, u32[]{:S(2)}, u32[]{:S(2)}) collective-permute-start(bf16[1,440,768]{2,1,0:T(8,128)(2,1)} %copy.313), channel_id=1, source_target_pairs={{0,2},{2,4},{4,6},{6,8},{8,10},{10,12},{12,14},{14,16},{16,18},{18... | collective-permute-start | bytes 2027528 | tf_op jit(solution)/shard_map/ppermute | solution.py:48
  1499.3 238.1 %copy-start.152 = (bf16[1,768,768]{2,1,0:T(8,128)(2,1)S(1)}, bf16[1,768,768]{2,1,0:T(8,128)(2,1)}, u32[]{:S(2)}) copy-start(bf16[1,768,768]{2,1,0:T(8,128)(2,1)} %param.29) | copy-start | bytes 3538948
  1787.9 259.0 %all-gather.5.cloned.1.call-start = ((), (), s32[]{:S(2)}) async-start(), calls=%async_computation.15 | async-start | bytes 16220160 | tf_op jit(solution)/shard_map/all_gather | solution.py:41
  1912.3 802.8 %all-reduce.19.cloned.1.call-start = ((), (), s32[]{:S(2)}) async-start(), calls=%async_computation.16 | async-start | bytes 3637248 | tf_op jit(solution)/shard_map/psum | solution.py:28
  2099.7 20.8 collective-permute-start.15
  2105.0 30.0 collective-permute-start.16
  2105.7 43.8 %collective-permute-start.17 = (bf16[1,440,768]{2,1,0:T(8,128)(2,1)S(1)}, bf16[1,440,768]{2,1,0:T(8,128)(2,1)}, u32[]{:S(2)}, u32[]{:S(2)}) collective-permute-start(bf16[1,440,768]{2,1,0:T(8,128)(2,1)S(1)} %copy.333), channel_id=1, source_target_pairs={{0,26},{2,28},{4,30},{6,0},{8,2},{10,4},{12,6},{14,8},{16,10},{18,... | collective-permute-start | bytes 2027528 | tf_op jit(solution)/shard_map/ppermute | solution.py:48
  2106.0 57.9 %collective-permute-start.18 = (bf16[1,440,768]{2,1,0:T(8,128)(2,1)S(1)}, bf16[1,440,768]{2,1,0:T(8,128)(2,1)}, u32[]{:S(2)}, u32[]{:S(2)}) collective-permute-start(bf16[1,440,768]{2,1,0:T(8,128)(2,1)S(1)} %copy.334), channel_id=1, source_target_pairs={{0,24},{2,26},{4,28},{6,30},{8,0},{10,2},{12,4},{14,6},{16,8},{18,... | collective-permute-start | bytes 2027528 | tf_op jit(solution)/shard_map/ppermute | solution.py:48
  2106.6 71.8 %collective-permute-start.19 = (bf16[1,440,768]{2,1,0:T(8,128)(2,1)S(1)}, bf16[1,440,768]{2,1,0:T(8,128)(2,1)}, u32[]{:S(2)}, u32[]{:S(2)}) collective-permute-start(bf16[1,440,768]{2,1,0:T(8,128)(2,1)S(1)} %copy.335), channel_id=1, source_target_pairs={{0,22},{2,24},{4,26},{6,28},{8,30},{10,0},{12,2},{14,4},{16,6},{18... | collective-permute-start | bytes 2027528 | tf_op jit(solution)/shard_map/ppermute | solution.py:48
  2120.5 72.5 %collective-permute-start.20 = (bf16[1,440,768]{2,1,0:T(8,128)(2,1)}, bf16[1,440,768]{2,1,0:T(8,128)(2,1)}, u32[]{:S(2)}, u32[]{:S(2)}) collective-permute-start(bf16[1,440,768]{2,1,0:T(8,128)(2,1)} %copy.336), channel_id=1, source_target_pairs={{0,20},{2,22},{4,24},{6,26},{8,28},{10,30},{12,0},{14,2},{16,4},{1... | collective-permute-start | bytes 2027528 | tf_op jit(solution)/shard_map/ppermute | solution.py:48
  2135.0 102.8 %collective-permute-start.21 = (bf16[1,440,768]{2,1,0:T(8,128)(2,1)}, bf16[1,440,768]{2,1,0:T(8,128)(2,1)}, u32[]{:S(2)}, u32[]{:S(2)}) collective-permute-start(bf16[1,440,768]{2,1,0:T(8,128)(2,1)} %copy.337), channel_id=1, source_target_pairs={{0,18},{2,20},{4,22},{6,24},{8,26},{10,28},{12,30},{14,0},{16,2},{... | collective-permute-start | bytes 2027528 | tf_op jit(solution)/shard_map/ppermute | solution.py:48
  2149.4 181.2 %collective-permute-start.22 = (bf16[1,440,768]{2,1,0:T(8,128)(2,1)}, bf16[1,440,768]{2,1,0:T(8,128)(2,1)}, u32[]{:S(2)}, u32[]{:S(2)}) collective-permute-start(bf16[1,440,768]{2,1,0:T(8,128)(2,1)} %copy.338), channel_id=1, source_target_pairs={{0,16},{2,18},{4,20},{6,22},{8,24},{10,26},{12,28},{14,30},{16,0},... | collective-permute-start | bytes 2027528 | tf_op jit(solution)/shard_map/ppermute | solution.py:48
  2163.9 166.8 %collective-permute-start.23 = (bf16[1,440,768]{2,1,0:T(8,128)(2,1)}, bf16[1,440,768]{2,1,0:T(8,128)(2,1)}, u32[]{:S(2)}, u32[]{:S(2)}) collective-permute-start(bf16[1,440,768]{2,1,0:T(8,128)(2,1)} %copy.339), channel_id=1, source_target_pairs={{0,14},{2,16},{4,18},{6,20},{8,22},{10,24},{12,26},{14,28},{16,30}... | collective-permute-start | bytes 2027528 | tf_op jit(solution)/shard_map/ppermute | solution.py:48
  2178.4 152.3 %collective-permute-start.24 = (bf16[1,440,768]{2,1,0:T(8,128)(2,1)}, bf16[1,440,768]{2,1,0:T(8,128)(2,1)}, u32[]{:S(2)}, u32[]{:S(2)}) collective-permute-start(bf16[1,440,768]{2,1,0:T(8,128)(2,1)} %copy.340), channel_id=1, source_target_pairs={{0,12},{2,14},{4,16},{6,18},{8,20},{10,22},{12,24},{14,26},{16,28}... | collective-permute-start | bytes 2027528 | tf_op jit(solution)/shard_map/ppermute | solution.py:48
  2180.1 151.1 %copy-start.64 = (f32[1182,2]{0,1:T(2,128)S(1)}, f32[1182,2]{0,1:T(2,128)}, u32[]{:S(2)}) copy-start(f32[1182,2]{0,1:T(2,128)} %copy-done.63) | copy-start | bytes 28372
  2180.1 151.1 %copy-start.71 = (f32[1182]{0:T(1024)S(1)}, f32[1182]{0:T(1024)}, u32[]{:S(2)}) copy-start(f32[1182]{0:T(1024)} %copy-done.70) | copy-start | bytes 14188
  2180.1 151.1 %copy-start.83 = (f32[1182]{0:T(1024)S(1)}, f32[1182]{0:T(1024)}, u32[]{:S(2)}) copy-start(f32[1182]{0:T(1024)} %copy-done.82) | copy-start | bytes 14188
  2180.1 151.1 %copy-start.88 = (s32[1182,2]{0,1:T(2,128)S(1)}, s32[1182,2]{0,1:T(2,128)}, u32[]{:S(2)}) copy-start(s32[1182,2]{0,1:T(2,128)} %param.19) | copy-start | bytes 28372
  2193.0 169.4 %collective-permute-start.25 = (bf16[1,440,768]{2,1,0:T(8,128)(2,1)S(1)}, bf16[1,440,768]{2,1,0:T(8,128)(2,1)S(1)}, u32[]{:S(2)}, u32[]{:S(2)}) collective-permute-start(bf16[1,440,768]{2,1,0:T(8,128)(2,1)S(1)} %copy.341), channel_id=1, source_target_pairs={{0,10},{2,12},{4,14},{6,16},{8,18},{10,20},{12,22},{14,24},{16,26}... | collective-permute-start | bytes 2027528 | tf_op jit(solution)/shard_map/ppermute | solution.py:48
  2237.8 126.9 %collective-permute-start.26 = (bf16[1,440,768]{2,1,0:T(8,128)(2,1)S(1)}, bf16[1,440,768]{2,1,0:T(8,128)(2,1)S(1)}, u32[]{:S(2)}, u32[]{:S(2)}) collective-permute-start(bf16[1,440,768]{2,1,0:T(8,128)(2,1)S(1)} %copy.342), channel_id=1, source_target_pairs={{0,8},{2,10},{4,12},{6,14},{8,16},{10,18},{12,20},{14,22},{16,24},... | collective-permute-start | bytes 2027528 | tf_op jit(solution)/shard_map/ppermute | solution.py:48
  2330.6 36.2 %collective-permute-start.27 = (bf16[1,440,768]{2,1,0:T(8,128)(2,1)S(1)}, bf16[1,440,768]{2,1,0:T(8,128)(2,1)S(1)}, u32[]{:S(2)}, u32[]{:S(2)}) collective-permute-start(bf16[1,440,768]{2,1,0:T(8,128)(2,1)S(1)} %copy.343), channel_id=1, source_target_pairs={{0,6},{2,8},{4,10},{6,12},{8,14},{10,16},{12,18},{14,20},{16,22},{... | collective-permute-start | bytes 2027528 | tf_op jit(solution)/shard_map/ppermute | solution.py:48
  2330.7 38.3 %collective-permute-start.28 = (bf16[1,440,768]{2,1,0:T(8,128)(2,1)S(1)}, bf16[1,440,768]{2,1,0:T(8,128)(2,1)S(1)}, u32[]{:S(2)}, u32[]{:S(2)}) collective-permute-start(bf16[1,440,768]{2,1,0:T(8,128)(2,1)S(1)} %copy.344), channel_id=1, source_target_pairs={{0,4},{2,6},{4,8},{6,10},{8,12},{10,14},{12,16},{14,18},{16,20},{1... | collective-permute-start | bytes 2027528 | tf_op jit(solution)/shard_map/ppermute | solution.py:48
  2330.7 40.5 %collective-permute-start.29 = (bf16[1,440,768]{2,1,0:T(8,128)(2,1)S(1)}, bf16[1,440,768]{2,1,0:T(8,128)(2,1)S(1)}, u32[]{:S(2)}, u32[]{:S(2)}) collective-permute-start(bf16[1,440,768]{2,1,0:T(8,128)(2,1)S(1)} %copy.345), channel_id=1, source_target_pairs={{0,2},{2,4},{4,6},{6,8},{8,10},{10,12},{12,14},{14,16},{16,18},{18... | collective-permute-start | bytes 2027528 | tf_op jit(solution)/shard_map/ppermute | solution.py:48
  2331.3 265.5 %copy-start.78 = (bf16[1182,8]{0,1:T(8,128)(2,1)}, bf16[1182,8]{0,1:T(8,128)(2,1)S(1)}, u32[]{:S(2)}) copy-start(bf16[1182,8]{0,1:T(8,128)(2,1)S(1)} %select_reduce_fusion.1) | copy-start | bytes 56740
  2657.5 62.1 %copy-start.94 = (f32[1182]{0:T(1024)S(1)}, f32[1182]{0:T(1024)}, u32[]{:S(2)}) copy-start(f32[1182]{0:T(1024)} %copy-done.93) | copy-start | bytes 14188
  2657.5 62.1 %copy-start.107 = (f32[1182]{0:T(1024)S(1)}, f32[1182]{0:T(1024)}, u32[]{:S(2)}) copy-start(f32[1182]{0:T(1024)} %copy-done.106) | copy-start | bytes 14188
  2657.5 136.9 %all-reduce.21.cloned.1.call-start = ((), (), s32[]{:S(2)}) async-start(), calls=%async_computation.17 | async-start | bytes 3637248 | tf_op jit(solution)/shard_map/psum | solution.py:28
  2737.4 180.1 %all-reduce.23.cloned.1.call-start = ((), (), s32[]{:S(2)}) async-start(), calls=%async_computation.18 | async-start | bytes 3637248 | tf_op jit(solution)/shard_map/psum | solution.py:28
  2860.5 116.7 %reduce-scatter.26.cloned.1.call-start = ((), (), s32[]{:S(2)}) async-start(), calls=%async_computation.23 | async-start | bytes 417792
  2863.5 179.3 %reduce-scatter.24.cloned.1.call-start = ((), (), s32[]{:S(2)}) async-start(), calls=%async_computation.22 | async-start | bytes 417792
  2927.1 167.2 %reduce-scatter.22.cloned.1.call-start = ((), (), s32[]{:S(2)}) async-start(), calls=%async_computation.21 | async-start | bytes 417792
  2930.1 352.4 %all-reduce.25.cloned.1.call-start = ((), (), s32[]{:S(2)}) async-start(), calls=%async_computation.24 | async-start | bytes 18874368
  2952.0 410.4 %reduce-scatter.20.cloned.1.call-start = ((), (), s32[]{:S(2)}) async-start(), calls=%async_computation.20 | async-start | bytes 5013504 | tf_op jit(solution)/shard_map/reduce_scatter | solution.py:263
  2962.0 479.8 %reduce-scatter.18.cloned.1.call-start = ((), (), s32[]{:S(2)}) async-start(), calls=%async_computation.19 | async-start | bytes 5013504 | tf_op jit(solution)/shard_map/reduce_scatter | solution.py:262
  (147 other events, 1263.7 us)
Sparse Core Ops, SparseCore 0:
  56.0 59.5 all-reduce.12
  132.0 56.8 all-reduce.14
  237.9 56.8 all-reduce.16
  604.0 124.8 reduce-scatter.13
  730.4 133.0 all-gather.2
  1788.0 124.1 reduce-scatter.15
  1913.8 133.1 all-gather.4
  2657.6 57.4 all-reduce.18
  2737.6 56.8 all-reduce.20
  2860.6 56.8 all-reduce.22
  2921.6 55.5 reduce-scatter.25
  2981.0 54.5 reduce-scatter.23
  3039.6 54.6 reduce-scatter.21
  3098.3 184.1 all-reduce.24
  3286.8 75.6 reduce-scatter.19
  3367.2 74.5 reduce-scatter.17
